TPU v7x, 32 devices: a whole 2x2x4 slice. The times are simulated.
32 devices in a mesh: rep: 4 (over z), shard: 8 (over y, x, core).
Axes of the slice: x: 2, y: 2, z: 4, core: 2. Of those that a mesh axis runs over, the one named last changes fastest.
Arguments:
- tokens: bfloat16 [8192, 1024], P(('rep', 'shard')), may hold values from -6 to 6
- prefix: int32 [32], P(('rep', 'shard')), may hold values from 25 to 128
- routes: int32 [8192, 8], P(('rep', 'shard')), may hold values from 0 to 31, all different within a row; in each aligned block of 256 rows (0 to 255, 256 to 511, ...) at most 96 rows name the same one
- cotangent: bfloat16 [8192, 1024], P(('rep', 'shard')), may hold values from -6 to 6
- w_query: bfloat16 [1024, 1024], P('shard'), may hold values from -0.625 to 0.625
- key_weight: bfloat16 [1024, 512], P('shard'), may hold values from -0.625 to 0.625
- value_weight: bfloat16 [1024, 512], P('shard'), may hold values from -0.1875 to 0.1875
- w_out: bfloat16 [1024, 1024], P('shard'), may hold values from -6 to 6
- norm_attn: bfloat16 [1024], P('shard'), may hold values from 0.5 to 1.5
- norm_moe: bfloat16 [1024], P('shard'), may hold values from 0.5 to 1.5
- w_router: bfloat16 [1024, 32], P('shard'), may hold values from -0.09375 to 0.09375
- w_gate: bfloat16 [32, 1024, 512], P('shard'), may hold values from -0.1875 to 0.1875
- w_up: bfloat16 [32, 1024, 512], P('shard'), may hold values from -0.1875 to 0.1875
- w_down: bfloat16 [32, 512, 1024], P('shard'), may hold values from -6 to 6
Outputs:
- layer_out: bfloat16 [8192, 1024], P(('rep', 'shard'))
- d_tokens: float32 [8192, 1024], P(('rep', 'shard'))
- d_w_query: float32 [1024, 1024], P('shard')
- d_w_key: float32 [1024, 512], P('shard')
- d_w_value: float32 [1024, 512], P('shard')
- d_w_out: float32 [1024, 1024], P('shard')
- d_norm_attn: float32 [1024], P('shard')
- d_norm_moe: float32 [1024], P('shard')
- d_w_router: float32 [1024, 32], P('shard')
- d_w_gate: float32 [32, 1024, 512], P('shard')
- d_w_up: float32 [32, 1024, 512], P('shard')
- d_w_down: float32 [32, 512, 1024], P('shard')
Inputs may be any that keep to these rules, and one draw needn't show every extreme that they name: `routes`: each row names 8 different experts; among the rows of one device no expert is named more than 96 times, and in every draw some device's rows name some expert exactly 96 times.
All inputs are finite; a program needn't handle non-finite values.
Results may differ from a plain program's by a relative error of at most 0.024.
Values may be sent and summed in bfloat16 or wider, within the bound.
A program may use at most 256 MiB of HBM per device.

v0:
```python
import math
import jax
import jax.numpy as jnp
from jax import lax
from jax.sharding import PartitionSpec as P

QUERY_HEADS = 16
KEY_VALUE_HEADS = 8
HEAD_SIZE = 64
CAP = 96
LANES = 128
MOST_GATHERED = 4
epsilon = 1e-06
score_scale = 0.015625
branch_scale = 0.22
masked_value = -1e30
f32 = jnp.float32
bf16 = jnp.bfloat16


def dot(left, right, contract=((1,), (0,))):
    return lax.dot_general(left, right, (contract, ((), ())), preferred_element_type=f32)


def norm_scale(rows):
    return lax.rsqrt(jnp.mean(rows * rows, axis=-1, keepdims=True) + epsilon)


def norm_backward(rows, scaling, gain, upstream):
    weighted = upstream * gain
    inner_mean = jnp.mean(weighted * rows, axis=-1, keepdims=True)
    gradient = scaling * weighted - rows * (scaling * scaling * scaling) * inner_mean
    return (gradient, jnp.sum(upstream * rows * scaling, axis=0, keepdims=True))


def rotary_tables(count):
    half = HEAD_SIZE // 2
    places = jnp.arange(count, dtype=f32)
    inverse = jnp.exp(jnp.arange(half, dtype=f32) * (-2.0 * math.log(10000.0) / HEAD_SIZE))
    angles = places[:, None] * inverse[None, :]
    return (jnp.cos(angles)[:, None, :], jnp.sin(angles)[:, None, :])


def apply_rotary(rows, cosine, sine):
    half = HEAD_SIZE // 2
    shaped = rows.reshape(rows.shape[0], -1, HEAD_SIZE)
    first, second = (shaped[..., :half], shaped[..., half:])
    turned = jnp.concatenate(
        [first * cosine - second * sine, second * cosine + first * sine], axis=-1
    )
    return turned.reshape(rows.shape)


def attention_scores(query, keys, prefix_len):
    count = query.shape[0]
    raw = jnp.einsum("tngd,snd->ngts", query, keys, preferred_element_type=f32)
    place = jnp.arange(count, dtype=jnp.int32)
    visible = (place[None, :] <= place[:, None]) | (place[None, :] < prefix_len)
    return jnp.where(visible, raw * score_scale, masked_value)


def slots_of(gates, first_expert, local):
    tokens = gates.shape[1]
    mine = lax.dynamic_slice_in_dim(gates, first_expert, local, axis=2)
    named = mine > 0
    place = jnp.arange(tokens)
    earlier = (place[None, :] < place[:, None]).astype(bf16)
    rank = jnp.einsum("ts,bsl->blt", earlier, named.astype(bf16), preferred_element_type=f32)
    slot = jnp.arange(CAP, dtype=f32)
    here = (rank[:, :, None, :] == slot[None, None, :, None]) & named.transpose(0, 2, 1)[
        :, :, None, :
    ]
    return (here, mine)


def body(
    tokens,
    prefix,
    routes,
    cotangent,
    w_query,
    key_weight,
    value_weight,
    w_out,
    norm_attn,
    norm_moe,
    w_router,
    w_gate,
    w_up,
    w_down,
):
    inputs = tokens.astype(f32)
    count, width = inputs.shape
    local, _, hidden = w_gate.shape
    shards, reps = (lax.axis_size("shard"), lax.axis_size("rep"))
    experts = local * shards
    kv_width = key_weight.shape[1]
    me, rep = (lax.axis_index("shard"), lax.axis_index("rep"))
    group = QUERY_HEADS // KEY_VALUE_HEADS
    small = jnp.concatenate([w_router, norm_attn[:, None], norm_moe[:, None]], axis=1)
    small = jnp.pad(small, ((0, 0), (0, LANES - small.shape[1])))
    packed = jnp.concatenate([w_query, key_weight, value_weight, w_out, small], axis=1)
    packed = lax.all_gather(packed, "shard", axis=0, tiled=True)
    cuts = [width, width + kv_width, width + 2 * kv_width, 2 * width + 2 * kv_width]
    wq, wk, wv, wo, small = jnp.split(packed, cuts, axis=1)
    wr = small[:, :experts]
    gain_one = small[:, experts].astype(f32)[None, :]
    gain_two = small[:, experts + 1].astype(f32)[None, :]
    spread = reps <= MOST_GATHERED
    axes = ("rep", "shard") if spread else "shard"
    all_cot = lax.all_gather(cotangent, axes, axis=0, tiled=True)
    scale_one = norm_scale(inputs)
    normed_one = (inputs * scale_one * gain_one).astype(bf16)
    cosine, sine = rotary_tables(count)
    query = apply_rotary(dot(normed_one, wq), cosine, sine).astype(bf16)
    keys = apply_rotary(dot(normed_one, wk), cosine, sine).astype(bf16)
    values = dot(normed_one, wv).astype(bf16)
    query4 = query.reshape(count, KEY_VALUE_HEADS, group, HEAD_SIZE)
    keys3 = keys.reshape(count, KEY_VALUE_HEADS, HEAD_SIZE)
    values3 = values.reshape(count, KEY_VALUE_HEADS, HEAD_SIZE)
    scores = attention_scores(query4, keys3, prefix[0])
    weights = jnp.exp(scores - jnp.max(scores, axis=-1, keepdims=True))
    probs = weights / jnp.sum(weights, axis=-1, keepdims=True)
    probs_low = probs.astype(bf16)
    attended = jnp.einsum("ngts,snd->tngd", probs_low, values3, preferred_element_type=f32)
    attended = attended.reshape(count, -1).astype(bf16)
    hidden_one = inputs + branch_scale * dot(attended, wo)
    scale_two = norm_scale(hidden_one)
    normed_two = (hidden_one * scale_two * gain_two).astype(bf16)
    logits = dot(normed_two, wr)
    picks = routes[:, :, None] == jnp.arange(experts, dtype=jnp.int32)[None, None, :]
    chosen_mask = jnp.any(picks, axis=1)
    top = jnp.max(jnp.where(chosen_mask, logits, -jnp.inf), axis=1, keepdims=True)
    gates = jnp.where(chosen_mask, jnp.exp(logits - top), 0.0)
    gates = gates / jnp.sum(gates, axis=1, keepdims=True)
    high = gates.astype(bf16)
    low = (gates - high.astype(f32)).astype(bf16)
    pad = jnp.zeros((count, LANES - 2 * experts), bf16)
    sent = jnp.concatenate([normed_two, high, low, pad], axis=1)
    arrived = lax.all_gather(sent, axes, axis=0, tiled=True)
    arrived = arrived.reshape(-1, shards, count, width + LANES)
    all_gates = arrived[..., width : width + experts].astype(f32)
    all_gates = all_gates + arrived[..., width + experts : width + 2 * experts].astype(f32)
    all_cot = all_cot.reshape(-1, shards, count, width)

    def gathered(number):
        rows = lax.dynamic_index_in_dim(arrived, number, 0, keepdims=False)[..., :width]
        cot = lax.dynamic_index_in_dim(all_cot, number, 0, keepdims=False)
        gate_rows = lax.dynamic_index_in_dim(all_gates, number, 0, keepdims=False)
        here, mine = slots_of(gate_rows, me * local, local)
        one_hot = here.astype(bf16)
        slot_gate = jnp.sum(jnp.where(here, mine.transpose(0, 2, 1)[:, :, None, :], 0.0), axis=3)
        xg = jnp.einsum("blst,btd->lbsd", one_hot, rows).reshape(local, -1, width)
        cg = jnp.einsum("blst,btd->lbsd", one_hot, cot).reshape(local, -1, width)
        scale = branch_scale * slot_gate.transpose(1, 0, 2).reshape(local, -1)[:, :, None]
        gate_part = jnp.einsum("lmd,ldf->lmf", xg, w_gate, preferred_element_type=f32)
        up_part = jnp.einsum("lmd,ldf->lmf", xg, w_up, preferred_element_type=f32)
        raw = jnp.einsum("lmd,lfd->lmf", cg, w_down, preferred_element_type=f32)
        sigma = jax.nn.sigmoid(gate_part)
        act = gate_part * sigma
        inner = act * up_part
        d_inner = raw * scale
        d_gate = (d_inner * up_part * sigma * (1.0 + gate_part * (1.0 - sigma))).astype(bf16)
        d_up = (d_inner * act).astype(bf16)
        scaled = (inner * scale).astype(bf16)
        sums = (
            jnp.einsum("lmd,lmf->ldf", xg, d_gate, preferred_element_type=f32),
            jnp.einsum("lmd,lmf->ldf", xg, d_up, preferred_element_type=f32),
            jnp.einsum("lmf,lmd->lfd", scaled, cg, preferred_element_type=f32),
        )
        return (sums, (one_hot, inner, raw, d_gate, d_up, scaled))

    sums, (one_hot, inner, raw, d_gate, d_up, scaled) = gathered(rep if spread else 0)
    out_rows = jnp.einsum("lmf,lfd->lmd", scaled, w_down, preferred_element_type=f32).astype(bf16)
    d_rows = jnp.einsum("lmf,ldf->lmd", d_gate, w_gate, preferred_element_type=f32)
    d_rows = (d_rows + jnp.einsum("lmf,ldf->lmd", d_up, w_up, preferred_element_type=f32)).astype(
        bf16
    )
    slot_d_gate = branch_scale * jnp.sum(inner * raw, axis=2)
    shape4 = (local, shards, CAP, width)
    mix = jnp.einsum(
        "blst,lbsd->btd", one_hot, out_rows.reshape(shape4), preferred_element_type=f32
    )
    d_in = jnp.einsum("blst,lbsd->btd", one_hot, d_rows.reshape(shape4), preferred_element_type=f32)
    dg_local = jnp.sum(
        jnp.where(
            one_hot > 0, slot_d_gate.reshape(local, shards, CAP).transpose(1, 0, 2)[..., None], 0.0
        ),
        axis=2,
    )
    dg = jnp.zeros((shards, count, LANES), f32)
    dg = lax.dynamic_update_slice(dg, dg_local.transpose(0, 2, 1), (0, 0, me * local))
    back = jnp.concatenate([mix, d_in, dg], axis=2).astype(bf16).reshape(shards * count, -1)
    back = lax.psum_scatter(back, "shard", scatter_dimension=0, tiled=True).astype(f32)
    if spread:
        for step in range(1, reps):
            more, _ = gathered(lax.rem(rep + step, reps))
            sums = tuple((a + b for a, b in zip(sums, more)))
    else:
        sums = tuple((lax.psum(a.astype(bf16), "rep").astype(f32) for a in sums))
    d_w_gate, d_w_up, d_w_down = sums
    result = (hidden_one + back[:, :width]).astype(bf16)
    cot = cotangent.astype(f32)
    d_gates = back[:, 2 * width : 2 * width + experts]
    d_logits = gates * (d_gates - jnp.sum(gates * d_gates, axis=1, keepdims=True))
    d_logits = d_logits.astype(bf16)
    d_router = dot(normed_two, d_logits, ((0,), (0,)))
    d_normed_two = back[:, width : 2 * width] + dot(d_logits, wr, ((1,), (1,)))
    d_hidden, d_gain_two = norm_backward(hidden_one, scale_two, gain_two, d_normed_two)
    d_hidden = d_hidden + cot
    d_projected = (branch_scale * d_hidden).astype(bf16)
    d_wo = dot(attended, d_projected, ((0,), (0,)))
    d_attended = dot(d_projected, wo, ((1,), (1,))).astype(bf16)
    d_attended = d_attended.reshape(count, KEY_VALUE_HEADS, group, HEAD_SIZE)
    d_values = jnp.einsum("ngts,tngd->snd", probs_low, d_attended, preferred_element_type=f32)
    d_probs = jnp.einsum("tngd,snd->ngts", d_attended, values3, preferred_element_type=f32)
    weighted = jnp.sum(probs * d_probs, axis=-1, keepdims=True)
    d_scores = (probs * (d_probs - weighted) * score_scale).astype(bf16)
    d_query = jnp.einsum("ngts,snd->tngd", d_scores, keys3, preferred_element_type=f32)
    d_keys = jnp.einsum("ngts,tngd->snd", d_scores, query4, preferred_element_type=f32)
    d_query = apply_rotary(d_query.reshape(count, -1), cosine, -sine).astype(bf16)
    d_keys = apply_rotary(d_keys.reshape(count, -1), cosine, -sine).astype(bf16)
    d_values = d_values.reshape(count, -1).astype(bf16)
    d_qkv = jnp.concatenate([d_query, d_keys, d_values], axis=1)
    d_w_qkv = dot(normed_one, d_qkv, ((0,), (0,)))
    d_normed_one = dot(d_qkv, packed[:, : cuts[2]], ((1,), (1,)))
    d_tokens, d_gain_one = norm_backward(inputs, scale_one, gain_one, d_normed_one)
    d_tokens = d_tokens + d_hidden
    small = jnp.concatenate([d_router, d_gain_one.T, d_gain_two.T], axis=1)
    small = jnp.pad(small, ((0, 0), (0, LANES - small.shape[1])))
    shares = jnp.concatenate([d_w_qkv, d_wo, small], axis=1).astype(bf16)
    shares = lax.psum_scatter(shares, "shard", scatter_dimension=0, tiled=True)
    totals = lax.psum(shares, "rep").astype(f32)
    d_wq, d_wk, d_wv, d_wo, small = jnp.split(totals, cuts, axis=1)
    return (
        result,
        d_tokens,
        d_wq,
        d_wk,
        d_wv,
        d_wo,
        small[:, experts],
        small[:, experts + 1],
        small[:, :experts],
        d_w_gate,
        d_w_up,
        d_w_down,
    )


def solution(mesh):
    rows = P(("rep", "shard"), None)
    one, two, three = (P("shard"), P("shard", None), P("shard", None, None))
    return jax.shard_map(
        body,
        mesh=mesh,
        in_specs=(
            rows,
            P(("rep", "shard")),
            rows,
            rows,
            two,
            two,
            two,
            two,
            one,
            one,
            two,
            three,
            three,
            three,
        ),
        out_specs=(rows, rows, two, two, two, two, one, one, two, three, three, three),
        check_vma=False,
    )
```

profile of v0, /device:TPU:0, one launch (start us, length us, event | category | flops | bytes accessed | tf_op | source)
XLA Modules:
  0.0 835.5 jit_solution(13934311828291077232)
XLA Ops:
  17.2 45.2 %all-gather.4.cloned.1.call-done = bf16[1024,3200]{1,0:T(8,128)(2,1)} async-done(((bf16[128,3200]{1,0:T(8,128)(2,1)}), bf16[1024,3200]{1,0:T(8,128)(2,1)}) %all-gather.4.cloned.1.call-update) | async-done | bytes 6553616 | tf_op jit(solution)/shard_map/all_gather | solution.py:103
  67.9 2.7 fusion.104
  70.8 3.4 fusion.228
  74.3 2.7 convolution_convert_fusion.3
  77.0 2.6 multiply_reduce_fusion.3
  85.2 124.0 %all-gather.6.cloned.1.call-done = bf16[8192,1152]{1,0:T(8,128)(2,1)} async-done(((bf16[256,1152]{1,0:T(8,128)(2,1)}), bf16[8192,1152]{1,0:T(8,128)(2,1)}) %all-gather.6.cloned.1.call-update) | async-done | bytes 18874384 | tf_op jit(solution)/shard_map/all_gather | solution.py:140
  209.2 3.1 convert_add_fusion
  218.9 13.0 %dynamic-slice_bitcast_fusion = (bf16[8,256,1152]{2,1,0:T(8,128)(2,1)}, bf16[8,256,1152]{2,1,0:T(8,128)(2,1)S(1)}, bf16[8,256,1152]{2,1,0:T(8,128)(2,1)}, bf16[8,256,1152]{2,1,0:T(8,128)(2,1)}) fusion(bf16[4,8,256,1152]{3,2,1,0:T(8,128)(2,1)} %bitcast.302, s32[]{:T(128)S(6)} %select_n.86, s32[]{:T(128)S(6)} %select_n.83, s32[]{:T(128)S(6)} %select_n.80, ...), kind=kLoop, calls=%fused_computation.37 | loop fusion | bytes 37748752 | tf_op jit(solution)/shard_map/jit(dynamic_index_in_dim)/squeeze | solution.py:147
  233.7 3.5 copy.406
  237.4 87.7 %all-gather.8.cloned.1.call-done = bf16[8192,1024]{1,0:T(8,128)(2,1)} async-done(((bf16[256,1024]{1,0:T(8,128)(2,1)}), bf16[8192,1024]{1,0:T(8,128)(2,1)}) %all-gather.8.cloned.1.call-update) | async-done | bytes 16777232 | tf_op jit(solution)/shard_map/all_gather | solution.py:111
  325.1 6.8 fusion.74
  331.9 6.8 fusion.79
  338.7 4.5 fusion.93
  343.2 4.1 copy.419
  347.3 5.5 fusion.242
  352.8 8.8 %fusion.239 = f32[4,768,512]{1,2,0:T(8,128)} fusion(bf16[4,768,1024]{2,1,0:T(8,128)(2,1)} %bitcast.319, bf16[4,1024,512]{2,1,0:T(8,128)(2,1)S(1)} %copy-done.9), kind=kOutput, calls=%fused_computation.296 | convolution fusion | flops 3221225472 | bytes 16777216 | tf_op jit(solution)/shard_map/lmd,ldf->lmf/dot_general | solution.py:156
  361.6 8.4 %fusion.241 = f32[4,768,512]{1,2,0:T(8,128)} fusion(bf16[4,768,1024]{2,1,0:T(8,128)(2,1)S(1)} %bitcast.308, bf16[4,1024,512]{2,1,0:T(8,128)(2,1)} %param.26), kind=kOutput, calls=%fused_computation.298 | convolution fusion | flops 3221225472 | bytes 16777216 | tf_op jit(solution)/shard_map/lmd,ldf->lmf/dot_general | solution.py:157
  370.0 10.2 %fusion.238 = f32[4,768,512]{1,2,0:T(8,128)} fusion(bf16[4,768,1024]{2,1,0:T(8,128)(2,1)} %bitcast.320, bf16[4,1024,512]{2,1,0:T(8,128)(2,1)} %param.26), kind=kOutput, calls=%fused_computation.295 | convolution fusion | flops 3221225472 | bytes 16777216 | tf_op jit(solution)/shard_map/lmd,ldf->lmf/dot_general | solution.py:157
  380.4 6.9 fusion.64
  387.3 4.5 fusion.84
  391.8 3.9 copy.369
  395.7 10.9 %fusion.230 = f32[4,768,512]{1,2,0:T(8,128)} fusion(bf16[4,768,1024]{2,1,0:T(8,128)(2,1)S(1)} %bitcast.295, bf16[4,1024,512]{2,1,0:T(8,128)(2,1)} %param.26), kind=kOutput, calls=%fused_computation.287 | convolution fusion | flops 3221225472 | bytes 16777216 | tf_op jit(solution)/shard_map/lmd,ldf->lmf/dot_general | solution.py:157
  406.6 5.4 fusion.229
  419.9 4.1 fusion.87
  424.1 3.9 copy.393
  428.0 3.3 copy.420
  431.3 3.5 copy.407
  434.8 3.5 copy.376
  438.3 15.0 %multiply_reduce_fusion = (f32[4,768]{1,0:T(4,128)S(1)}, f32[4,768,512]{1,2,0:T(8,128)}) fusion(f32[4,768,512]{1,2,0:T(8,128)} %fusion.230, f32[4,768,512]{1,2,0:T(8,128)} %fusion.229, bf16[4,768,1024]{2,1,0:T(8,128)(2,1)S(1)} %bitcast.299, bf16[4,512,1024]{2,1,0:T(8,128)(2,1)} %param.27), kind=kOutput, calls=%fused_computation.31 | convolution fusion | flops 3232232448 | bytes 29372416 | tf_op jit(solution)/shard_map/lmd,lfd->lmf/dot_general | solution.py:158
  456.7 8.4 %multiply_convert_fusion.11 = (bf16[4,768,512]{1,2,0:T(8,128)(2,1)S(1)}, bf16[4,768,512]{1,2,0:T(8,128)(2,1)S(1)}, bf16[4,768,512]{1,2,0:T(8,128)(2,1)S(1)}) fusion(f32[4,768]{1,0:T(4,128)S(1)} %mul.709, f32[4,768,512]{1,2,0:T(8,128)} %fusion.230, f32[4,768,512]{1,2,0:T(8,128)} %fusion.229, f32[4,768,512]{1,2,0:T(8,128)} %get-tuple-element.124), kind=kLoop, calls=%fused_computation.34 | loop fusion | flops 26738688 | bytes 28323840 | tf_op jit(solution)/shard_map/convert_element_type | solution.py:165
  465.1 5.6 convolution_convert_fusion.1
  470.7 7.3 bitcast_convert_fusion.1
  478.1 6.7 fusion.231
  484.8 9.6 %add_convert_fusion = bf16[4,768,1024]{2,1,0:T(8,128)(2,1)} fusion(f32[4,768,1024]{2,1,0:T(8,128)} %fusion.231, bf16[4,768,512]{1,2,0:T(8,128)(2,1)S(1)} %get-tuple-element.91, bf16[4,1024,512]{2,1,0:T(8,128)(2,1)} %param.26), kind=kOutput, calls=%fused_computation.4 | convolution fusion | flops 3227516928 | bytes 26214400 | tf_op jit(solution)/shard_map/lmf,ldf->lmd/dot_general | solution.py:176
  494.4 7.2 bitcast_convert_fusion
  503.5 7.1 pad_maximum_fusion
  510.8 4.2 fusion.69
  515.0 4.1 copy.394
  520.6 5.8 fusion.236
  526.4 8.7 %fusion.235 = f32[4,768,512]{1,2,0:T(8,128)} fusion(bf16[4,768,1024]{2,1,0:T(8,128)(2,1)S(1)} %bitcast.328, bf16[4,1024,512]{2,1,0:T(8,128)(2,1)} %param.26), kind=kOutput, calls=%fused_computation.292 | convolution fusion | flops 3221225472 | bytes 16777216 | tf_op jit(solution)/shard_map/lmd,ldf->lmf/dot_general | solution.py:157
  535.2 11.0 %fusion.234 = f32[4,768,512]{1,2,0:T(8,128)} fusion(bf16[4,768,1024]{2,1,0:T(8,128)(2,1)} %bitcast.329, bf16[4,512,1024]{2,1,0:T(8,128)(2,1)} %param.27), kind=kOutput, calls=%fused_computation.291 | convolution fusion | flops 3221225472 | bytes 16777216 | tf_op jit(solution)/shard_map/lmd,lfd->lmf/dot_general | solution.py:158
  546.2 8.4 %fusion.237 = f32[4,768,512]{1,2,0:T(8,128)} fusion(bf16[4,768,1024]{2,1,0:T(8,128)(2,1)} %bitcast.335, bf16[4,512,1024]{2,1,0:T(8,128)(2,1)S(1)} %copy-done.52), kind=kOutput, calls=%fused_computation.294 | convolution fusion | flops 3221225472 | bytes 16777216 | tf_op jit(solution)/shard_map/lmd,lfd->lmf/dot_general | solution.py:158
  554.6 5.5 fusion.240
  560.1 12.0 %fusion.39 = f32[4,512,1024]{2,1,0:T(8,128)} fusion(bf16[4,768,1024]{2,1,0:T(8,128)(2,1)S(1)} %bitcast.334, f32[4,768,512]{1,2,0:T(8,128)} %fusion.241, f32[4,768]{1,0:T(4,128)S(1)} %mul.780, f32[4,768,512]{1,2,0:T(8,128)} %fusion.242), kind=kOutput, calls=%fused_computation.79 | convolution fusion | flops 3232235520 | bytes 27275264 | tf_op jit(solution)/shard_map/lmf,lmd->lfd/dot_general | solution.py:169
  572.0 13.2 %fusion.38 = f32[4,512,1024]{2,1,0:T(8,128)} fusion(bf16[4,768,1024]{2,1,0:T(8,128)(2,1)} %bitcast.336, f32[4,768,512]{1,2,0:T(8,128)} %fusion.238, f32[4,768]{1,0:T(4,128)S(1)} %copy-done.45, f32[4,768,512]{1,2,0:T(8,128)} %fusion.239), kind=kOutput, calls=%fused_computation.78 | convolution fusion | flops 3232235520 | bytes 27275264 | tf_op jit(solution)/shard_map/lmf,lmd->lfd/dot_general | solution.py:169
  585.3 14.5 %fusion.35 = f32[4,1024,512]{2,1,0:T(8,128)} fusion(bf16[4,768,1024]{2,1,0:T(8,128)(2,1)} %bitcast.321, f32[4,768,512]{1,2,0:T(8,128)} %fusion.237, f32[4,768]{1,0:T(4,128)S(1)} %copy-done.45, f32[4,768,512]{1,2,0:T(8,128)} %fusion.239), kind=kOutput, calls=%fused_computation.75 | convolution fusion | flops 3232235520 | bytes 27275264 | tf_op jit(solution)/shard_map/lmd,lmf->ldf/dot_general | solution.py:168
  599.8 14.7 %fusion.36 = f32[4,1024,512]{2,1,0:T(8,128)} fusion(bf16[4,768,1024]{2,1,0:T(8,128)(2,1)} %bitcast.309, f32[4,768,512]{1,2,0:T(8,128)} %fusion.240, f32[4,768]{1,0:T(4,128)S(1)} %mul.780, f32[4,768,512]{1,2,0:T(8,128)} %fusion.242), kind=kOutput, calls=%fused_computation.76 | convolution fusion | flops 3232235520 | bytes 27275264 | tf_op jit(solution)/shard_map/lmd,lmf->ldf/dot_general | solution.py:168
  614.5 14.4 %fusion.34 = f32[4,1024,512]{2,1,0:T(8,128)} fusion(bf16[4,768,1024]{2,1,0:T(8,128)(2,1)} %bitcast.323, f32[4,768,512]{1,2,0:T(8,128)} %fusion.234, f32[4,768]{1,0:T(4,128)S(1)} %copy-done.43, f32[4,768,512]{1,2,0:T(8,128)} %fusion.236), kind=kOutput, calls=%fused_computation.74 | convolution fusion | flops 3232235520 | bytes 27275264 | tf_op jit(solution)/shard_map/lmd,lmf->ldf/dot_general | solution.py:168
  637.7 3.7 fusion.145
  641.5 2.9 fusion.232
  644.4 8.0 fusion.144
  652.4 8.2 fusion.111
  662.9 4.4 convolution_convert_fusion
  667.4 4.5 fusion.160
  672.1 5.6 fusion.3
  678.4 14.6 %fusion.37 = f32[4,512,1024]{2,1,0:T(8,128)} fusion(bf16[4,768,1024]{2,1,0:T(8,128)(2,1)} %bitcast.330, f32[4,768,512]{1,2,0:T(8,128)} %fusion.235, f32[4,768]{1,0:T(4,128)S(1)} %copy-done.44, f32[4,768,512]{1,2,0:T(8,128)} %fusion.236), kind=kOutput, calls=%fused_computation.77 | convolution fusion | flops 3232235520 | bytes 27275264 | tf_op jit(solution)/shard_map/lmf,lmd->lfd/dot_general | solution.py:169
  693.1 9.8 %fusion.233 = f32[4,1024,512]{2,1,0:T(8,128)} fusion(bf16[4,768,1024]{2,1,0:T(8,128)(2,1)} %bitcast.297, bf16[4,768,512]{1,2,0:T(8,128)(2,1)S(1)} %copy-done.6), kind=kOutput, calls=%fused_computation.290 | convolution fusion | flops 3221225472 | bytes 17825792 | tf_op jit(solution)/shard_map/lmd,lmf->ldf/dot_general | solution.py:167
  702.8 17.3 %fusion.47 = f32[4,1024,512]{2,1,0:T(8,128)} fusion(bf16[4,768,1024]{2,1,0:T(8,128)(2,1)} %bitcast.322, f32[4,768,512]{1,2,0:T(8,128)} %fusion.239, f32[4,768,512]{1,2,0:T(8,128)} %fusion.238, f32[4,768,512]{1,2,0:T(8,128)} %fusion.237, f32[4,768]{1,0:T(4,128)S(1)} %copy-done.46), kind=kOutput, calls=%fused_computation.96 | convolution fusion | flops 3238526976 | bytes 33566720 | tf_op jit(solution)/shard_map/lmd,lmf->ldf/dot_general | solution.py:167
  720.2 17.0 %fusion.46 = f32[4,1024,512]{2,1,0:T(8,128)} fusion(bf16[4,768,1024]{2,1,0:T(8,128)(2,1)} %bitcast.324, f32[4,768,512]{1,2,0:T(8,128)} %fusion.236, f32[4,768,512]{1,2,0:T(8,128)} %fusion.235, f32[4,768,512]{1,2,0:T(8,128)} %fusion.234, f32[4,768]{1,0:T(4,128)S(1)} %copy-done.44), kind=kOutput, calls=%fused_computation.95 | convolution fusion | flops 3238526976 | bytes 33566720 | tf_op jit(solution)/shard_map/lmd,lmf->ldf/dot_general | solution.py:167
  737.2 15.8 %add_add_fusion = f32[4,512,1024]{2,1,0:T(8,128)} fusion(f32[4,512,1024]{2,1,0:T(8,128)} %fusion.39, f32[4,512,1024]{2,1,0:T(8,128)} %fusion.38, f32[4,512,1024]{2,1,0:T(8,128)} %fusion.37, bf16[4,768,512]{1,2,0:T(8,128)(2,1)S(1)} %copy-done.8, bf16[4,768,1024]{2,1,0:T(8,128)(2,1)} %bitcast.300), kind=kOutput, calls=%fused_computation.8 | convolution fusion | flops 3227516928 | bytes 42991616 | tf_op jit(solution)/shard_map/lmf,lmd->lfd/dot_general | solution.py:169
  753.0 21.8 %add_add_fusion.2 = f32[4,1024,512]{2,1,0:T(8,128)} fusion(f32[4,1024,512]{2,1,0:T(8,128)} %fusion.47, f32[4,1024,512]{2,1,0:T(8,128)} %fusion.233, f32[4,1024,512]{2,1,0:T(8,128)} %fusion.46, bf16[4,768,1024]{2,1,0:T(8,128)(2,1)} %bitcast.310, f32[4,768,512]{1,2,0:T(8,128)} %fusion.242, f32[4,768,512]{1,2,0:T(8,128)} %fusion.241, ...), kind=kOutput, calls=%fused_computation.10 | convolution fusion | flops 3244818432 | bytes 58732544 | tf_op jit(solution)/shard_map/lmd,lmf->ldf/dot_general | solution.py:167
  774.8 15.5 %add_add_fusion.1 = f32[4,1024,512]{2,1,0:T(8,128)} fusion(f32[4,1024,512]{2,1,0:T(8,128)} %fusion.36, f32[4,1024,512]{2,1,0:T(8,128)} %fusion.35, f32[4,1024,512]{2,1,0:T(8,128)} %fusion.34, bf16[4,768,1024]{2,1,0:T(8,128)(2,1)} %bitcast.298, bf16[4,768,512]{1,2,0:T(8,128)(2,1)S(1)} %copy-done.3), kind=kOutput, calls=%fused_computation.9 | convolution fusion | flops 3227516928 | bytes 42991616 | tf_op jit(solution)/shard_map/lmd,lmf->ldf/dot_general | solution.py:168
  790.3 3.0 fusion.157
  793.3 27.6 %all-reduce.4.cloned.1.call-done = bf16[128,3200]{1,0:T(8,128)(2,1)} async-done(((bf16[128,3200]{1,0:T(8,128)(2,1)}), bf16[128,3200]{1,0:T(8,128)(2,1)}) %all-reduce.4.cloned.1.call-update) | async-done | bytes 819216 | tf_op jit(solution)/shard_map/psum | solution.py:233
  (259 shorter events, 63.1 us)
Async XLA Ops:
  7.2 58.7 %copy-start.19 = (bf16[256,1024]{1,0:T(8,128)(2,1)S(1)}, bf16[256,1024]{1,0:T(8,128)(2,1)}, u32[]{:S(2)}) copy-start(bf16[256,1024]{1,0:T(8,128)(2,1)} %param.14) | copy-start | bytes 1572868
  7.2 55.2 %all-gather.4.cloned.1.call-start = ((), (), s32[]{:S(2)}) async-start(), calls=%async_computation.2 | async-start | bytes 7372800 | tf_op jit(solution)/shard_map/all_gather | solution.py:103
  12.9 196.3 %all-gather.6.cloned.1.call-start = ((), (), s32[]{:S(2)}) async-start(), calls=%async_computation.3 | async-start | bytes 19464192 | tf_op jit(solution)/shard_map/all_gather | solution.py:140
  16.3 54.5 %copy-start.48 = (f32[256]{0:T(256)}, f32[256]{0:T(256)S(1)}, u32[]{:S(2)}) copy-start(f32[256]{0:T(256)S(1)} %get-tuple-element.111) | copy-start | bytes 3076
  17.2 53.5 %copy-start.25 = (f32[256,32]{0,1:T(8,128)}, f32[256,32]{0,1:T(8,128)S(1)}, u32[]{:S(2)}) copy-start(f32[256,32]{0,1:T(8,128)S(1)} %get-tuple-element.116) | copy-start | bytes 98308
  63.8 7.0 copy-start.39
  63.8 16.5 %copy-start.37 = (f32[1024]{0:T(1024)}, f32[1024]{0:T(1024)S(1)}, u32[]{:S(2)}) copy-start(f32[1024]{0:T(1024)S(1)} %get-tuple-element.72) | copy-start | bytes 12292
  65.8 8.4 %copy-start.23 = (bf16[256,512]{0,1:T(8,128)(2,1)}, bf16[256,512]{0,1:T(8,128)(2,1)S(1)}, u32[]{:S(2)}) copy-start(bf16[256,512]{0,1:T(8,128)(2,1)S(1)} %copy.360) | copy-start | bytes 786436
  67.9 6.4 copy-start.33
  67.9 6.4 copy-start.35
  70.8 6.2 copy-start.29
  77.0 5.2 copy-start.27
  80.3 128.9 %copy-start.41 = (f32[256]{0:T(256)}, f32[256]{0:T(256)S(1)}, u32[]{:S(2)}) copy-start(f32[256]{0:T(256)S(1)} %get-tuple-element.113) | copy-start | bytes 3076
  80.8 134.1 %copy-start.15 = (bf16[256,1024]{1,0:T(8,128)(2,1)}, bf16[256,1024]{1,0:T(8,128)(2,1)S(1)}, u32[]{:S(2)}) copy-start(bf16[256,1024]{1,0:T(8,128)(2,1)S(1)} %multiply_convert_fusion.24) | copy-start | bytes 1572868
  84.3 240.8 %all-gather.8.cloned.1.call-start = ((), (), s32[]{:S(2)}) async-start(), calls=%async_computation.4 | async-start | bytes 17301504 | tf_op jit(solution)/shard_map/all_gather | solution.py:111
  85.1 543.8 %reduce-scatter.3.cloned.1.call-start = ((), (), s32[]{:S(2)}) async-start(), calls=%async_computation.5 | async-start | bytes 10027008 | tf_op jit(solution)/shard_map/reduce_scatter | solution.py:194
  325.1 13.6 %slice-start.10 = ((s8[4718592]{0:T(1024)(128)(4,1)}), s8[4194304]{0:T(1024)(128)(4,1)S(1)}, s32[]{:S(2)}) async-start(s8[4718592]{0:T(1024)(128)(4,1)} %bitcast.340), calls=%async_computation.18 | async-start | bytes 8388608
  331.9 6.8 slice-start.11
  343.2 4.1 copy-start.9
  347.3 14.3 %copy-start.4 = (bf16[4,8,96,1024]{3,2,1,0:T(8,128)(2,1)}, bf16[4,8,96,1024]{3,2,1,0:T(8,128)(2,1)S(1)}, u32[]{:S(2)}) copy-start(bf16[4,8,96,1024]{3,2,1,0:T(8,128)(2,1)S(1)} %copy.419) | copy-start | bytes 18874372
  380.2 7.1 slice-start.8
  380.4 6.9 slice-start.9
  395.7 10.9 %copy-start = (bf16[4,8,96,1024]{3,2,1,0:T(8,128)(2,1)}, bf16[4,8,96,1024]{3,2,1,0:T(8,128)(2,1)S(1)}, u32[]{:S(2)}) copy-start(bf16[4,8,96,1024]{3,2,1,0:T(8,128)(2,1)S(1)} %copy.369) | copy-start | bytes 18874372
  419.9 8.1 slice-start.2
  424.1 7.3 slice-start
  438.3 15.0 %copy-start.1 = (bf16[4,8,96,1024]{3,2,1,0:T(8,128)(2,1)}, bf16[4,8,96,1024]{3,2,1,0:T(8,128)(2,1)S(1)}, u32[]{:S(2)}) copy-start(bf16[4,8,96,1024]{3,2,1,0:T(8,128)(2,1)S(1)} %copy.376) | copy-start | bytes 18874372
  456.7 8.5 %copy-start.51 = (bf16[4,512,1024]{2,1,0:T(8,128)(2,1)S(1)}, bf16[4,512,1024]{2,1,0:T(8,128)(2,1)}, u32[]{:S(2)}) copy-start(bf16[4,512,1024]{2,1,0:T(8,128)(2,1)} %param.27) | copy-start | bytes 12582916
  465.1 5.6 copy-start.7
  465.1 13.0 %copy-start.5 = (bf16[4,768,512]{1,2,0:T(8,128)(2,1)}, bf16[4,768,512]{1,2,0:T(8,128)(2,1)S(1)}, u32[]{:S(2)}) copy-start(bf16[4,768,512]{1,2,0:T(8,128)(2,1)S(1)} %get-tuple-element.90) | copy-start | bytes 9437188
  465.1 19.7 %copy-start.2 = (bf16[4,768,512]{1,2,0:T(8,128)(2,1)}, bf16[4,768,512]{1,2,0:T(8,128)(2,1)S(1)}, u32[]{:S(2)}) copy-start(bf16[4,768,512]{1,2,0:T(8,128)(2,1)S(1)} %get-tuple-element.91) | copy-start | bytes 9437188
  470.7 7.3 copy-start.10
  494.4 7.3 copy-start.18
  510.7 264.1 %reduce-scatter.5.cloned.1.call-start = ((), (), s32[]{:S(2)}) async-start(), calls=%async_computation.6 | async-start | bytes 7372800 | tf_op jit(solution)/shard_map/reduce_scatter | solution.py:232
  510.8 8.3 slice-start.4
  514.9 4.2 copy-start.11
  515.0 5.6 slice-start.5
  535.2 11.0 %copy-start.52 = (bf16[4,512,1024]{2,1,0:T(8,128)(2,1)S(1)}, bf16[4,512,1024]{2,1,0:T(8,128)(2,1)}, u32[]{:S(2)}) copy-start(bf16[4,512,1024]{2,1,0:T(8,128)(2,1)} %param.27) | copy-start | bytes 12582916
  535.2 19.4 %slice-start.6 = ((s8[6291456]{0:T(1024)(128)(4,1)}), s8[4194304]{0:T(1024)(128)(4,1)S(1)}, s32[]{:S(2)}) async-start(s8[6291456]{0:T(1024)(128)(4,1)} %bitcast.331), calls=%async_computation.14 | async-start | bytes 8388608
  546.2 8.4 %slice-start.7 = ((s8[6291456]{0:T(1024)(128)(4,1)}), s8[2097152]{0:T(1024)(128)(4,1)S(1)}, s32[]{:S(2)}) async-start(s8[6291456]{0:T(1024)(128)(4,1)} %bitcast.331), calls=%async_computation.15 | async-start | bytes 4194304
  560.1 12.0 %copy-start.45 = (f32[4,768]{1,0:T(4,128)S(1)}, f32[4,768]{1,0:T(4,128)}, u32[]{:S(2)}) copy-start(f32[4,768]{1,0:T(4,128)} %mul.771) | copy-start | bytes 36868
  599.8 14.7 %copy-start.43 = (f32[4,768]{1,0:T(4,128)S(1)}, f32[4,768]{1,0:T(4,128)}, u32[]{:S(2)}) copy-start(f32[4,768]{1,0:T(4,128)} %mul.762) | copy-start | bytes 36868
  614.5 15.9 %copy-start.22 = (f32[256,32]{1,0:T(8,128)S(1)}, f32[256,32]{1,0:T(8,128)}, u32[]{:S(2)}) copy-start(f32[256,32]{1,0:T(8,128)} %get-tuple-element.84) | copy-start | bytes 98308
  614.5 16.2 %copy-start.16 = (bf16[256,1024]{1,0:T(8,128)(2,1)S(1)}, bf16[256,1024]{1,0:T(8,128)(2,1)}, u32[]{:S(2)}) copy-start(bf16[256,1024]{1,0:T(8,128)(2,1)} %copy-done.15) | copy-start | bytes 1572868
  614.5 16.4 %copy-start.14 = (f32[256,1024]{1,0:T(8,128)S(1)}, f32[256,1024]{1,0:T(8,128)}, u32[]{:S(2)}) copy-start(f32[256,1024]{1,0:T(8,128)} %copy-done.13) | copy-start | bytes 3145732
  614.5 16.4 %copy-start.38 = (f32[1024]{0:T(1024)S(1)}, f32[1024]{0:T(1024)}, u32[]{:S(2)}) copy-start(f32[1024]{0:T(1024)} %copy-done.37) | copy-start | bytes 12292
  614.5 16.4 %copy-start.42 = (f32[256]{0:T(256)S(1)}, f32[256]{0:T(256)}, u32[]{:S(2)}) copy-start(f32[256]{0:T(256)} %copy-done.41) | copy-start | bytes 3076
  628.9 5.3 copy-start.28
  632.9 4.8 copy-start.55
  637.7 6.7 copy-start.30
  644.4 8.0 copy-start.34
  644.4 8.0 copy-start.36
  652.4 9.0 %copy-start.26 = (f32[256,32]{0,1:T(8,128)S(1)}, f32[256,32]{0,1:T(8,128)}, u32[]{:S(2)}) copy-start(f32[256,32]{0,1:T(8,128)} %copy-done.25) | copy-start | bytes 98308
  652.4 9.0 %copy-start.31 = (f32[256,8,64]{0,2,1:T(8,128)S(1)}, f32[256,8,64]{0,2,1:T(8,128)}, u32[]{:S(2)}) copy-start(f32[256,8,64]{0,2,1:T(8,128)} %fusion.144) | copy-start | bytes 1572868
  652.4 9.0 %copy-start.32 = (f32[256,32]{0,1:T(8,128)S(1)}, f32[256,32]{0,1:T(8,128)}, u32[]{:S(2)}) copy-start(f32[256,32]{0,1:T(8,128)} %get-tuple-element.114) | copy-start | bytes 98308
  652.4 10.5 %copy-start.20 = (bf16[256,1024]{1,0:T(8,128)(2,1)S(1)}, bf16[256,1024]{1,0:T(8,128)(2,1)}, u32[]{:S(2)}) copy-start(bf16[256,1024]{1,0:T(8,128)(2,1)} %param.14) | copy-start | bytes 1572868
  652.4 10.5 %copy-start.40 = (f32[1024]{0:T(1024)S(1)}, f32[1024]{0:T(1024)}, u32[]{:S(2)}) copy-start(f32[1024]{0:T(1024)} %copy-done.39) | copy-start | bytes 12292
  660.7 6.7 copy-start.49
  660.7 6.7 copy-start.53
  677.7 15.3 %copy-start.6 = (bf16[4,768,512]{1,2,0:T(8,128)(2,1)S(1)}, bf16[4,768,512]{1,2,0:T(8,128)(2,1)}, u32[]{:S(2)}) copy-start(bf16[4,768,512]{1,2,0:T(8,128)(2,1)} %copy-done.5) | copy-start | bytes 9437188
  677.8 143.1 %all-reduce.4.cloned.1.call-start = ((), (), s32[]{:S(2)}) async-start(), calls=%async_computation.7 | async-start | bytes 1638400 | tf_op jit(solution)/shard_map/psum | solution.py:233
  693.1 9.8 %copy-start.46 = (f32[4,768]{1,0:T(4,128)S(1)}, f32[4,768]{1,0:T(4,128)}, u32[]{:S(2)}) copy-start(f32[4,768]{1,0:T(4,128)} %mul.771) | copy-start | bytes 36868
  720.2 17.0 %copy-start.8 = (bf16[4,768,512]{1,2,0:T(8,128)(2,1)S(1)}, bf16[4,768,512]{1,2,0:T(8,128)(2,1)}, u32[]{:S(2)}) copy-start(bf16[4,768,512]{1,2,0:T(8,128)(2,1)} %copy-done.7) | copy-start | bytes 9437188
  753.0 21.8 %copy-start.3 = (bf16[4,768,512]{1,2,0:T(8,128)(2,1)S(1)}, bf16[4,768,512]{1,2,0:T(8,128)(2,1)}, u32[]{:S(2)}) copy-start(bf16[4,768,512]{1,2,0:T(8,128)(2,1)} %copy-done.2) | copy-start | bytes 9437188
  774.8 15.5 %copy-start.47 = (f32[256]{0:T(256)S(1)}, f32[256]{0:T(256)}, u32[]{:S(2)}) copy-start(f32[256]{0:T(256)} %get-tuple-element.110) | copy-start | bytes 3076
  (10 other events, 25.4 us)
Sparse Core Ops, SparseCore 0:
  13.0 49.3 all-gather.3
  84.5 124.6 all-gather.5
  212.0 113.0 all-gather.7
  510.8 74.1 reduce-scatter.2
  677.9 63.5 reduce-scatter.4
  774.9 45.9 all-reduce.3
where the time goes:
time: 844 us; the launch traced here: 835 us
  matrix products  415 us (49%)
  waiting for transfers between devices  285 us (34%)
  local copies, waits for them, and re-layouts  73.7 us (9%)
  other arithmetic  45.3 us (5%)
  between operations  16.3 us (2%)
    all_gather x1, waiting for transfers between devices, body(): arrived = lax.all_gather(sent, axes, axis=0, tiled=True)  124 us
    all_gather x1, waiting for transfers between devices, body(): all_cot = lax.all_gather(cotangent, axes, axis=0, tiled=True)  87.7 us
    dot_general x4, matrix products, gathered(): jnp.einsum('lmd,lmf->ldf', xg, d_gate, preferred_element_type=f32)  65.9 us
    dot_general x4, matrix products, gathered(): jnp.einsum('lmd,lmf->ldf', xg, d_up, preferred_element_type=f32)  59 us
    dot_general x4, matrix products, gathered(): jnp.einsum('lmf,lmd->lfd', scaled, cg, preferred_element_type=f32)  55.6 us
    all_gather x1, waiting for transfers between devices, body(): packed = lax.all_gather(packed, 'shard', axis=0, tiled=True)  45.2 us
    dot_general x4, matrix products, gathered(): raw = jnp.einsum('lmd,lfd->lmf', cg, w_down, preferred_element_type=f32)  39.8 us
    dot_general x4, matrix products, gathered(): up_part = jnp.einsum('lmd,ldf->lmf', xg, w_up, preferred_element_type=f32)  38.2 us
  transfers between devices with their start and end apart: 6, of which 4 were waited for; matrix products, arithmetic and copies ran while one was open for 31% of the time, Pallas kernels for 0%

commit v1 on v0

--- a/solution.py
+++ b/solution.py
@@ -100,7 +100,14 @@
     small = jnp.concatenate([w_router, norm_attn[:, None], norm_moe[:, None]], axis=1)
     small = jnp.pad(small, ((0, 0), (0, LANES - small.shape[1])))
     packed = jnp.concatenate([w_query, key_weight, value_weight, w_out, small], axis=1)
-    packed = lax.all_gather(packed, "shard", axis=0, tiled=True)
+    ring = [packed]
+    for hop in range(7):
+        ring.append(lax.ppermute(ring[-1], "shard", [(dev, (dev + 1) % 8) for dev in range(8)]))
+    packed = jnp.roll(
+        jnp.concatenate(ring[::-1], axis=0),
+        (lax.axis_index("shard") + 1) * ring[0].shape[0],
+        axis=0,
+    )
     cuts = [width, width + kv_width, width + 2 * kv_width, 2 * width + 2 * kv_width]
     wq, wk, wv, wo, small = jnp.split(packed, cuts, axis=1)
     wr = small[:, :experts]

time: 844 us -> 890 us (1.055)
  waiting for transfers between devices: 285 us -> 326 us
  local copies, waits for them, and re-layouts: 73.7 us -> 82.9 us
    ppermute x0 -> x7, waiting for transfers between devices: none -> 85.2 us  [body(): lax.ppermute(ring[-1], 'shard', [(dev, (dev + 1) % 8) for dev in range(8)])]
    all_gather x1 -> x0, waiting for transfers between devices: 45.2 us -> none  [body(): packed = lax.all_gather(packed, 'shard', axis=0, tiled=True)]
    unnamed x142 -> x179, local copies, waits for them, and re-layouts: 8.41 us -> 18.8 us
  transfers between devices with their start and end apart: 6 -> 12, of which waited for: 4 -> 10; matrix products, arithmetic and copies ran while one was open for 31% -> 30% of each run, Pallas kernels for 0% -> 0%
where the time goes in v1:
time: 890 us; the launch traced here: 882 us
  matrix products  411 us (46%)
  waiting for transfers between devices  326 us (37%)
  local copies, waits for them, and re-layouts  82.9 us (9%)
  other arithmetic  44.1 us (5%)
  between operations  16.2 us (2%)
    all_gather x1, waiting for transfers between devices, body(): arrived = lax.all_gather(sent, axes, axis=0, tiled=True)  125 us
    all_gather x1, waiting for transfers between devices, body(): all_cot = lax.all_gather(cotangent, axes, axis=0, tiled=True)  88 us
    ppermute x7, waiting for transfers between devices, body(): lax.ppermute(ring[-1], 'shard', [(dev, (dev + 1) % 8) for dev in range(8)])  85.2 us
    dot_general x4, matrix products, gathered(): jnp.einsum('lmd,lmf->ldf', xg, d_gate, preferred_element_type=f32)  65.9 us
    dot_general x4, matrix products, gathered(): jnp.einsum('lmd,lmf->ldf', xg, d_up, preferred_element_type=f32)  58.8 us
    dot_general x4, matrix products, gathered(): jnp.einsum('lmf,lmd->lfd', scaled, cg, preferred_element_type=f32)  55.7 us
    dot_general x4, matrix products, gathered(): raw = jnp.einsum('lmd,lfd->lmf', cg, w_down, preferred_element_type=f32)  39.8 us
    dot_general x4, matrix products, gathered(): up_part = jnp.einsum('lmd,ldf->lmf', xg, w_up, preferred_element_type=f32)  38.3 us
  transfers between devices with their start and end apart: 12, of which 10 were waited for; matrix products, arithmetic and copies ran while one was open for 30% of the time, Pallas kernels for 0%

profile of v1, /device:TPU:0, one launch (start us, length us, event | category | flops | bytes accessed | tf_op | source)
XLA Modules:
  0.0 881.5 jit_solution(5889228728113937763)
XLA Ops:
  12.4 12.9 %collective-permute-done = bf16[128,3200]{1,0:T(8,128)(2,1)S(1)} collective-permute-done((bf16[128,3200]{1,0:T(8,128)(2,1)S(1)}, bf16[128,3200]{1,0:T(8,128)(2,1)S(1)}, u32[]{:S(2)}, u32[]{:S(2)}) %collective-permute-start) | collective-permute-done | bytes 819232 | tf_op jit(solution)/shard_map/ppermute | solution.py:105
  25.3 12.7 %collective-permute-done.1 = bf16[128,3200]{1,0:T(8,128)(2,1)S(1)} collective-permute-done((bf16[128,3200]{1,0:T(8,128)(2,1)S(1)}, bf16[128,3200]{1,0:T(8,128)(2,1)S(1)}, u32[]{:S(2)}, u32[]{:S(2)}) %collective-permute-start.1) | collective-permute-done | bytes 819232 | tf_op jit(solution)/shard_map/ppermute | solution.py:105
  38.0 12.7 %collective-permute-done.2 = bf16[128,3200]{1,0:T(8,128)(2,1)S(1)} collective-permute-done((bf16[128,3200]{1,0:T(8,128)(2,1)S(1)}, bf16[128,3200]{1,0:T(8,128)(2,1)S(1)}, u32[]{:S(2)}, u32[]{:S(2)}) %collective-permute-start.2) | collective-permute-done | bytes 819232 | tf_op jit(solution)/shard_map/ppermute | solution.py:105
  50.7 12.7 %collective-permute-done.3 = bf16[128,3200]{1,0:T(8,128)(2,1)S(1)} collective-permute-done((bf16[128,3200]{1,0:T(8,128)(2,1)S(1)}, bf16[128,3200]{1,0:T(8,128)(2,1)S(1)}, u32[]{:S(2)}, u32[]{:S(2)}) %collective-permute-start.3) | collective-permute-done | bytes 819232 | tf_op jit(solution)/shard_map/ppermute | solution.py:105
  64.2 12.8 %collective-permute-done.4 = bf16[128,3200]{1,0:T(8,128)(2,1)} collective-permute-done((bf16[128,3200]{1,0:T(8,128)(2,1)S(1)}, bf16[128,3200]{1,0:T(8,128)(2,1)}, u32[]{:S(2)}, u32[]{:S(2)}) %collective-permute-start.4) | collective-permute-done | bytes 819232 | tf_op jit(solution)/shard_map/ppermute | solution.py:105
  78.6 11.4 %collective-permute-done.5 = bf16[128,3200]{1,0:T(8,128)(2,1)} collective-permute-done((bf16[128,3200]{1,0:T(8,128)(2,1)}, bf16[128,3200]{1,0:T(8,128)(2,1)}, u32[]{:S(2)}, u32[]{:S(2)}) %collective-permute-start.5) | collective-permute-done | bytes 819232 | tf_op jit(solution)/shard_map/ppermute | solution.py:105
  92.7 10.2 %collective-permute-done.6 = bf16[128,3200]{1,0:T(8,128)(2,1)S(1)} collective-permute-done((bf16[128,3200]{1,0:T(8,128)(2,1)}, bf16[128,3200]{1,0:T(8,128)(2,1)S(1)}, u32[]{:S(2)}, u32[]{:S(2)}) %collective-permute-start.6) | collective-permute-done | bytes 819232 | tf_op jit(solution)/shard_map/ppermute | solution.py:105
  118.0 3.5 fusion.230
  132.7 124.9 %all-gather.3.cloned.1.call-done = bf16[8192,1152]{1,0:T(8,128)(2,1)} async-done(((bf16[256,1152]{1,0:T(8,128)(2,1)}), bf16[8192,1152]{1,0:T(8,128)(2,1)}) %all-gather.3.cloned.1.call-update) | async-done | bytes 18874384 | tf_op jit(solution)/shard_map/all_gather | solution.py:147
  267.4 12.8 %dynamic-slice_bitcast_fusion = (bf16[8,256,1152]{2,1,0:T(8,128)(2,1)}, bf16[8,256,1152]{2,1,0:T(8,128)(2,1)S(1)}, bf16[8,256,1152]{2,1,0:T(8,128)(2,1)}, bf16[8,256,1152]{2,1,0:T(8,128)(2,1)}) fusion(bf16[4,8,256,1152]{3,2,1,0:T(8,128)(2,1)} %bitcast.302, s32[]{:T(128)S(6)} %select_n.101, s32[]{:T(128)S(6)} %select_n.98, s32[]{:T(128)S(6)} %select_n.95, ...), kind=kLoop, calls=%fused_computation.37 | loop fusion | bytes 37748752 | tf_op jit(solution)/shard_map/jit(dynamic_index_in_dim)/squeeze | solution.py:154
  281.9 3.3 copy.406
  285.5 88.0 %all-gather.5.cloned.1.call-done = bf16[8192,1024]{1,0:T(8,128)(2,1)} async-done(((bf16[256,1024]{1,0:T(8,128)(2,1)}), bf16[8192,1024]{1,0:T(8,128)(2,1)}) %all-gather.5.cloned.1.call-update) | async-done | bytes 16777232 | tf_op jit(solution)/shard_map/all_gather | solution.py:118
  373.5 6.8 fusion.74
  380.3 6.7 fusion.79
  387.0 4.5 fusion.93
  391.5 4.1 copy.419
  395.6 5.4 fusion.244
  401.0 8.7 fusion.241
  409.8 8.4 fusion.243
  418.1 10.2 %fusion.240 = f32[4,768,512]{1,2,0:T(8,128)} fusion(bf16[4,768,1024]{2,1,0:T(8,128)(2,1)} %bitcast.320, bf16[4,1024,512]{2,1,0:T(8,128)(2,1)} %param.26), kind=kOutput, calls=%fused_computation.321 | convolution fusion | flops 3221225472 | bytes 16777216 | tf_op jit(solution)/shard_map/lmd,ldf->lmf/dot_general | solution.py:164
  428.5 6.9 fusion.64
  435.4 4.5 fusion.84
  439.9 3.9 copy.369
  443.8 10.9 %fusion.232 = f32[4,768,512]{1,2,0:T(8,128)} fusion(bf16[4,768,1024]{2,1,0:T(8,128)(2,1)S(1)} %bitcast.295, bf16[4,1024,512]{2,1,0:T(8,128)(2,1)} %param.26), kind=kOutput, calls=%fused_computation.313 | convolution fusion | flops 3221225472 | bytes 16777216 | tf_op jit(solution)/shard_map/lmd,ldf->lmf/dot_general | solution.py:164
  454.7 5.4 fusion.231
  468.0 4.1 fusion.87
  472.2 3.9 copy.393
  476.1 3.3 copy.420
  479.4 3.3 copy.407
  482.8 3.5 copy.376
  486.3 15.0 %multiply_reduce_fusion = (f32[4,768]{1,0:T(4,128)S(1)}, f32[4,768,512]{1,2,0:T(8,128)}) fusion(f32[4,768,512]{1,2,0:T(8,128)} %fusion.232, f32[4,768,512]{1,2,0:T(8,128)} %fusion.231, bf16[4,768,1024]{2,1,0:T(8,128)(2,1)S(1)} %bitcast.299, bf16[4,512,1024]{2,1,0:T(8,128)(2,1)} %param.27), kind=kOutput, calls=%fused_computation.31 | convolution fusion | flops 3232232448 | bytes 29372416 | tf_op jit(solution)/shard_map/lmd,lfd->lmf/dot_general | solution.py:165
  504.6 8.4 multiply_convert_fusion.11
  513.1 5.6 convolution_convert_fusion.1
  518.7 7.3 bitcast_convert_fusion.1
  526.0 6.8 fusion.233
  532.9 9.6 %add_convert_fusion = bf16[4,768,1024]{2,1,0:T(8,128)(2,1)} fusion(f32[4,768,1024]{2,1,0:T(8,128)} %fusion.233, bf16[4,768,512]{1,2,0:T(8,128)(2,1)S(1)} %get-tuple-element.91, bf16[4,1024,512]{2,1,0:T(8,128)(2,1)} %param.26), kind=kOutput, calls=%fused_computation.4 | convolution fusion | flops 3227516928 | bytes 26214400 | tf_op jit(solution)/shard_map/lmf,ldf->lmd/dot_general | solution.py:183
  542.5 7.2 bitcast_convert_fusion
  551.6 7.1 pad_maximum_fusion
  558.8 4.2 fusion.69
  563.0 4.1 copy.394
  568.6 5.9 fusion.238
  574.5 8.8 %fusion.237 = f32[4,768,512]{1,2,0:T(8,128)} fusion(bf16[4,768,1024]{2,1,0:T(8,128)(2,1)S(1)} %bitcast.328, bf16[4,1024,512]{2,1,0:T(8,128)(2,1)} %param.26), kind=kOutput, calls=%fused_computation.318 | convolution fusion | flops 3221225472 | bytes 16777216 | tf_op jit(solution)/shard_map/lmd,ldf->lmf/dot_general | solution.py:164
  583.3 11.0 %fusion.236 = f32[4,768,512]{1,2,0:T(8,128)} fusion(bf16[4,768,1024]{2,1,0:T(8,128)(2,1)} %bitcast.329, bf16[4,512,1024]{2,1,0:T(8,128)(2,1)} %param.27), kind=kOutput, calls=%fused_computation.317 | convolution fusion | flops 3221225472 | bytes 16777216 | tf_op jit(solution)/shard_map/lmd,lfd->lmf/dot_general | solution.py:165
  594.4 8.2 fusion.239
  602.6 5.5 fusion.242
  608.2 11.9 %fusion.39 = f32[4,512,1024]{2,1,0:T(8,128)} fusion(bf16[4,768,1024]{2,1,0:T(8,128)(2,1)S(1)} %bitcast.334, f32[4,768,512]{1,2,0:T(8,128)} %fusion.243, f32[4,768]{1,0:T(4,128)S(1)} %mul.784, f32[4,768,512]{1,2,0:T(8,128)} %fusion.244), kind=kOutput, calls=%fused_computation.79 | convolution fusion | flops 3232235520 | bytes 27275264 | tf_op jit(solution)/shard_map/lmf,lmd->lfd/dot_general | solution.py:176
  620.1 13.3 %fusion.38 = f32[4,512,1024]{2,1,0:T(8,128)} fusion(bf16[4,768,1024]{2,1,0:T(8,128)(2,1)} %bitcast.336, f32[4,768,512]{1,2,0:T(8,128)} %fusion.240, f32[4,768]{1,0:T(4,128)S(1)} %copy-done.51, f32[4,768,512]{1,2,0:T(8,128)} %fusion.241), kind=kOutput, calls=%fused_computation.78 | convolution fusion | flops 3232235520 | bytes 27275264 | tf_op jit(solution)/shard_map/lmf,lmd->lfd/dot_general | solution.py:176
  633.4 14.4 %fusion.35 = f32[4,1024,512]{2,1,0:T(8,128)} fusion(bf16[4,768,1024]{2,1,0:T(8,128)(2,1)} %bitcast.321, f32[4,768,512]{1,2,0:T(8,128)} %fusion.239, f32[4,768]{1,0:T(4,128)S(1)} %copy-done.51, f32[4,768,512]{1,2,0:T(8,128)} %fusion.241), kind=kOutput, calls=%fused_computation.75 | convolution fusion | flops 3232235520 | bytes 27275264 | tf_op jit(solution)/shard_map/lmd,lmf->ldf/dot_general | solution.py:175
  647.8 14.7 %fusion.36 = f32[4,1024,512]{2,1,0:T(8,128)} fusion(bf16[4,768,1024]{2,1,0:T(8,128)(2,1)} %bitcast.309, f32[4,768,512]{1,2,0:T(8,128)} %fusion.242, f32[4,768]{1,0:T(4,128)S(1)} %mul.784, f32[4,768,512]{1,2,0:T(8,128)} %fusion.244), kind=kOutput, calls=%fused_computation.76 | convolution fusion | flops 3232235520 | bytes 27275264 | tf_op jit(solution)/shard_map/lmd,lmf->ldf/dot_general | solution.py:175
  662.5 14.3 %fusion.34 = f32[4,1024,512]{2,1,0:T(8,128)} fusion(bf16[4,768,1024]{2,1,0:T(8,128)(2,1)} %bitcast.323, f32[4,768,512]{1,2,0:T(8,128)} %fusion.236, f32[4,768]{1,0:T(4,128)S(1)} %copy-done.49, f32[4,768,512]{1,2,0:T(8,128)} %fusion.238), kind=kOutput, calls=%fused_computation.74 | convolution fusion | flops 3232235520 | bytes 27275264 | tf_op jit(solution)/shard_map/lmd,lmf->ldf/dot_general | solution.py:175
  685.9 3.7 fusion.145
  692.6 8.1 fusion.144
  700.7 8.3 fusion.111
  710.6 4.6 fusion.160
  715.2 3.5 convolution_convert_fusion
  718.9 5.5 fusion.3
  725.1 14.6 %fusion.37 = f32[4,512,1024]{2,1,0:T(8,128)} fusion(bf16[4,768,1024]{2,1,0:T(8,128)(2,1)} %bitcast.330, f32[4,768,512]{1,2,0:T(8,128)} %fusion.237, f32[4,768]{1,0:T(4,128)S(1)} %copy-done.50, f32[4,768,512]{1,2,0:T(8,128)} %fusion.238), kind=kOutput, calls=%fused_computation.77 | convolution fusion | flops 3232235520 | bytes 27275264 | tf_op jit(solution)/shard_map/lmf,lmd->lfd/dot_general | solution.py:176
  739.7 9.7 %fusion.235 = f32[4,1024,512]{2,1,0:T(8,128)} fusion(bf16[4,768,1024]{2,1,0:T(8,128)(2,1)} %bitcast.297, bf16[4,768,512]{1,2,0:T(8,128)(2,1)S(1)} %copy-done.6), kind=kOutput, calls=%fused_computation.316 | convolution fusion | flops 3221225472 | bytes 17825792 | tf_op jit(solution)/shard_map/lmd,lmf->ldf/dot_general | solution.py:174
  749.5 17.3 %fusion.47 = f32[4,1024,512]{2,1,0:T(8,128)} fusion(bf16[4,768,1024]{2,1,0:T(8,128)(2,1)} %bitcast.322, f32[4,768,512]{1,2,0:T(8,128)} %fusion.241, f32[4,768,512]{1,2,0:T(8,128)} %fusion.240, f32[4,768,512]{1,2,0:T(8,128)} %fusion.239, f32[4,768]{1,0:T(4,128)S(1)} %copy-done.52), kind=kOutput, calls=%fused_computation.96 | convolution fusion | flops 3238526976 | bytes 33566720 | tf_op jit(solution)/shard_map/lmd,lmf->ldf/dot_general | solution.py:174
  766.8 17.1 %fusion.46 = f32[4,1024,512]{2,1,0:T(8,128)} fusion(bf16[4,768,1024]{2,1,0:T(8,128)(2,1)} %bitcast.324, f32[4,768,512]{1,2,0:T(8,128)} %fusion.238, f32[4,768,512]{1,2,0:T(8,128)} %fusion.237, f32[4,768,512]{1,2,0:T(8,128)} %fusion.236, f32[4,768]{1,0:T(4,128)S(1)} %copy-done.50), kind=kOutput, calls=%fused_computation.95 | convolution fusion | flops 3238526976 | bytes 33566720 | tf_op jit(solution)/shard_map/lmd,lmf->ldf/dot_general | solution.py:174
  783.9 15.8 %add_add_fusion = f32[4,512,1024]{2,1,0:T(8,128)} fusion(f32[4,512,1024]{2,1,0:T(8,128)} %fusion.39, f32[4,512,1024]{2,1,0:T(8,128)} %fusion.38, f32[4,512,1024]{2,1,0:T(8,128)} %fusion.37, bf16[4,768,512]{1,2,0:T(8,128)(2,1)S(1)} %copy-done.8, bf16[4,768,1024]{2,1,0:T(8,128)(2,1)} %bitcast.300), kind=kOutput, calls=%fused_computation.8 | convolution fusion | flops 3227516928 | bytes 42991616 | tf_op jit(solution)/shard_map/lmf,lmd->lfd/dot_general | solution.py:176
  799.7 21.8 %add_add_fusion.2 = f32[4,1024,512]{2,1,0:T(8,128)} fusion(f32[4,1024,512]{2,1,0:T(8,128)} %fusion.47, f32[4,1024,512]{2,1,0:T(8,128)} %fusion.235, f32[4,1024,512]{2,1,0:T(8,128)} %fusion.46, bf16[4,768,1024]{2,1,0:T(8,128)(2,1)} %bitcast.310, f32[4,768,512]{1,2,0:T(8,128)} %fusion.244, f32[4,768,512]{1,2,0:T(8,128)} %fusion.243, ...), kind=kOutput, calls=%fused_computation.10 | convolution fusion | flops 3244818432 | bytes 58732544 | tf_op jit(solution)/shard_map/lmd,lmf->ldf/dot_general | solution.py:174
  821.5 15.4 %add_add_fusion.1 = f32[4,1024,512]{2,1,0:T(8,128)} fusion(f32[4,1024,512]{2,1,0:T(8,128)} %fusion.36, f32[4,1024,512]{2,1,0:T(8,128)} %fusion.35, f32[4,1024,512]{2,1,0:T(8,128)} %fusion.34, bf16[4,768,1024]{2,1,0:T(8,128)(2,1)} %bitcast.298, bf16[4,768,512]{1,2,0:T(8,128)(2,1)S(1)} %copy-done.3), kind=kOutput, calls=%fused_computation.9 | convolution fusion | flops 3227516928 | bytes 42991616 | tf_op jit(solution)/shard_map/lmd,lmf->ldf/dot_general | solution.py:175
  840.0 27.3 %all-reduce.4.cloned.1.call-done = bf16[128,3200]{1,0:T(8,128)(2,1)} async-done(((bf16[128,3200]{1,0:T(8,128)(2,1)}), bf16[128,3200]{1,0:T(8,128)(2,1)}) %all-reduce.4.cloned.1.call-update) | async-done | bytes 819216 | tf_op jit(solution)/shard_map/psum | solution.py:240
  (308 shorter events, 86.8 us)
Async XLA Ops:
  7.2 250.4 %all-gather.3.cloned.1.call-start = ((), (), s32[]{:S(2)}) async-start(), calls=%async_computation.2 | async-start | bytes 19464192 | tf_op jit(solution)/shard_map/all_gather | solution.py:147
  11.9 95.2 %copy-start.22 = (bf16[128,1024]{1,0:T(8,128)(2,1)S(1)}, bf16[128,1024]{1,0:T(8,128)(2,1)}, u32[]{:S(2)}) copy-start(bf16[128,1024]{1,0:T(8,128)(2,1)} %param.18) | copy-start | bytes 786436
  11.9 13.4 %collective-permute-start = (bf16[128,3200]{1,0:T(8,128)(2,1)S(1)}, bf16[128,3200]{1,0:T(8,128)(2,1)S(1)}, u32[]{:S(2)}, u32[]{:S(2)}) collective-permute-start(bf16[128,3200]{1,0:T(8,128)(2,1)S(1)} %constant_dynamic-update-slice_fusion), channel_id=1, source_target_pairs={{0,1},{1,2},{2,3},{3,4},{4,5},{5,6},{6,7},{7,0},{8,9},{9,10},{10,1... | collective-permute-start | bytes 2457608 | tf_op jit(solution)/shard_map/ppermute | solution.py:105
  25.3 12.7 %collective-permute-start.1 = (bf16[128,3200]{1,0:T(8,128)(2,1)S(1)}, bf16[128,3200]{1,0:T(8,128)(2,1)S(1)}, u32[]{:S(2)}, u32[]{:S(2)}) collective-permute-start(bf16[128,3200]{1,0:T(8,128)(2,1)S(1)} %collective-permute-done), channel_id=1, source_target_pairs={{0,1},{1,2},{2,3},{3,4},{4,5},{5,6},{6,7},{7,0},{8,9},{9,10},{10,1... | collective-permute-start | bytes 2457608 | tf_op jit(solution)/shard_map/ppermute | solution.py:105
  38.0 12.7 %collective-permute-start.2 = (bf16[128,3200]{1,0:T(8,128)(2,1)S(1)}, bf16[128,3200]{1,0:T(8,128)(2,1)S(1)}, u32[]{:S(2)}, u32[]{:S(2)}) collective-permute-start(bf16[128,3200]{1,0:T(8,128)(2,1)S(1)} %collective-permute-done.1), channel_id=1, source_target_pairs={{0,1},{1,2},{2,3},{3,4},{4,5},{5,6},{6,7},{7,0},{8,9},{9,10},{10,1... | collective-permute-start | bytes 2457608 | tf_op jit(solution)/shard_map/ppermute | solution.py:105
  50.7 12.7 %collective-permute-start.3 = (bf16[128,3200]{1,0:T(8,128)(2,1)S(1)}, bf16[128,3200]{1,0:T(8,128)(2,1)S(1)}, u32[]{:S(2)}, u32[]{:S(2)}) collective-permute-start(bf16[128,3200]{1,0:T(8,128)(2,1)S(1)} %collective-permute-done.2), channel_id=1, source_target_pairs={{0,1},{1,2},{2,3},{3,4},{4,5},{5,6},{6,7},{7,0},{8,9},{9,10},{10,1... | collective-permute-start | bytes 2457608 | tf_op jit(solution)/shard_map/ppermute | solution.py:105
  64.2 12.8 %collective-permute-start.4 = (bf16[128,3200]{1,0:T(8,128)(2,1)S(1)}, bf16[128,3200]{1,0:T(8,128)(2,1)}, u32[]{:S(2)}, u32[]{:S(2)}) collective-permute-start(bf16[128,3200]{1,0:T(8,128)(2,1)S(1)} %collective-permute-done.3), channel_id=1, source_target_pairs={{0,1},{1,2},{2,3},{3,4},{4,5},{5,6},{6,7},{7,0},{8,9},{9,10},{10,1... | collective-permute-start | bytes 2457608 | tf_op jit(solution)/shard_map/ppermute | solution.py:105
  77.0 13.0 %collective-permute-start.5 = (bf16[128,3200]{1,0:T(8,128)(2,1)}, bf16[128,3200]{1,0:T(8,128)(2,1)}, u32[]{:S(2)}, u32[]{:S(2)}) collective-permute-start(bf16[128,3200]{1,0:T(8,128)(2,1)} %collective-permute-done.4), channel_id=1, source_target_pairs={{0,1},{1,2},{2,3},{3,4},{4,5},{5,6},{6,7},{7,0},{8,9},{9,10},{10,1... | collective-permute-start | bytes 2457608 | tf_op jit(solution)/shard_map/ppermute | solution.py:105
  78.5 28.5 %copy-start.26 = (bf16[128,512]{1,0:T(8,128)(2,1)S(1)}, bf16[128,512]{1,0:T(8,128)(2,1)}, u32[]{:S(2)}) copy-start(bf16[128,512]{1,0:T(8,128)(2,1)} %param.19) | copy-start | bytes 393220
  90.0 12.9 %collective-permute-start.6 = (bf16[128,3200]{1,0:T(8,128)(2,1)}, bf16[128,3200]{1,0:T(8,128)(2,1)S(1)}, u32[]{:S(2)}, u32[]{:S(2)}) collective-permute-start(bf16[128,3200]{1,0:T(8,128)(2,1)} %collective-permute-done.5), channel_id=1, source_target_pairs={{0,1},{1,2},{2,3},{3,4},{4,5},{5,6},{6,7},{7,0},{8,9},{9,10},{10,1... | collective-permute-start | bytes 2457608 | tf_op jit(solution)/shard_map/ppermute | solution.py:105
  91.2 15.9 %copy-start.27 = (bf16[128,512]{1,0:T(8,128)(2,1)S(1)}, bf16[128,512]{1,0:T(8,128)(2,1)}, u32[]{:S(2)}) copy-start(bf16[128,512]{1,0:T(8,128)(2,1)} %param.20) | copy-start | bytes 393220
  91.8 24.0 %copy-start.53 = (f32[256]{0:T(256)}, f32[256]{0:T(256)S(1)}, u32[]{:S(2)}) copy-start(f32[256]{0:T(256)S(1)} %get-tuple-element.111) | copy-start | bytes 3076
  91.9 15.3 %copy-start.23 = (bf16[128,1024]{1,0:T(8,128)(2,1)S(1)}, bf16[128,1024]{1,0:T(8,128)(2,1)}, u32[]{:S(2)}) copy-start(bf16[128,1024]{1,0:T(8,128)(2,1)} %param.21) | copy-start | bytes 786436
  92.7 25.1 %copy-start.31 = (f32[256,32]{0,1:T(8,128)}, f32[256,32]{0,1:T(8,128)S(1)}, u32[]{:S(2)}) copy-start(f32[256,32]{0,1:T(8,128)S(1)} %get-tuple-element.116) | copy-start | bytes 98308
  110.8 10.8 %copy-start.45 = (f32[1024]{0:T(1024)}, f32[1024]{0:T(1024)S(1)}, u32[]{:S(2)}) copy-start(f32[1024]{0:T(1024)S(1)} %get-tuple-element.73) | copy-start | bytes 12292
  110.8 16.8 %copy-start.43 = (f32[1024]{0:T(1024)}, f32[1024]{0:T(1024)S(1)}, u32[]{:S(2)}) copy-start(f32[1024]{0:T(1024)S(1)} %get-tuple-element.72) | copy-start | bytes 12292
  117.8 6.5 copy-start.39
  117.8 6.5 copy-start.41
  127.6 133.1 %copy-start.47 = (f32[256]{0:T(256)}, f32[256]{0:T(256)S(1)}, u32[]{:S(2)}) copy-start(f32[256]{0:T(256)S(1)} %get-tuple-element.113) | copy-start | bytes 3076
  128.1 135.1 %copy-start.15 = (bf16[256,1024]{1,0:T(8,128)(2,1)}, bf16[256,1024]{1,0:T(8,128)(2,1)S(1)}, u32[]{:S(2)}) copy-start(bf16[256,1024]{1,0:T(8,128)(2,1)S(1)} %multiply_convert_fusion.24) | copy-start | bytes 1572868
  131.7 241.8 %all-gather.5.cloned.1.call-start = ((), (), s32[]{:S(2)}) async-start(), calls=%async_computation.3 | async-start | bytes 17301504 | tf_op jit(solution)/shard_map/all_gather | solution.py:118
  132.5 544.4 %reduce-scatter.3.cloned.1.call-start = ((), (), s32[]{:S(2)}) async-start(), calls=%async_computation.4 | async-start | bytes 10027008 | tf_op jit(solution)/shard_map/reduce_scatter | solution.py:201
  373.5 13.4 %slice-start.10 = ((s8[4718592]{0:T(1024)(128)(4,1)}), s8[4194304]{0:T(1024)(128)(4,1)S(1)}, s32[]{:S(2)}) async-start(s8[4718592]{0:T(1024)(128)(4,1)} %bitcast.340), calls=%async_computation.17 | async-start | bytes 8388608
  380.3 6.7 slice-start.11
  395.6 14.2 %copy-start.4 = (bf16[4,8,96,1024]{3,2,1,0:T(8,128)(2,1)}, bf16[4,8,96,1024]{3,2,1,0:T(8,128)(2,1)S(1)}, u32[]{:S(2)}) copy-start(bf16[4,8,96,1024]{3,2,1,0:T(8,128)(2,1)S(1)} %copy.419) | copy-start | bytes 18874372
  428.3 7.1 slice-start.8
  428.5 6.9 slice-start.9
  443.8 10.9 %copy-start = (bf16[4,8,96,1024]{3,2,1,0:T(8,128)(2,1)}, bf16[4,8,96,1024]{3,2,1,0:T(8,128)(2,1)S(1)}, u32[]{:S(2)}) copy-start(bf16[4,8,96,1024]{3,2,1,0:T(8,128)(2,1)S(1)} %copy.369) | copy-start | bytes 18874372
  468.0 8.1 slice-start.2
  472.2 7.3 slice-start
  486.3 15.0 %copy-start.1 = (bf16[4,8,96,1024]{3,2,1,0:T(8,128)(2,1)}, bf16[4,8,96,1024]{3,2,1,0:T(8,128)(2,1)S(1)}, u32[]{:S(2)}) copy-start(bf16[4,8,96,1024]{3,2,1,0:T(8,128)(2,1)S(1)} %copy.376) | copy-start | bytes 18874372
  504.6 8.5 copy-start.58
  513.1 13.0 %copy-start.5 = (bf16[4,768,512]{1,2,0:T(8,128)(2,1)}, bf16[4,768,512]{1,2,0:T(8,128)(2,1)S(1)}, u32[]{:S(2)}) copy-start(bf16[4,768,512]{1,2,0:T(8,128)(2,1)S(1)} %get-tuple-element.90) | copy-start | bytes 9437188
  513.1 19.8 %copy-start.2 = (bf16[4,768,512]{1,2,0:T(8,128)(2,1)}, bf16[4,768,512]{1,2,0:T(8,128)(2,1)S(1)}, u32[]{:S(2)}) copy-start(bf16[4,768,512]{1,2,0:T(8,128)(2,1)S(1)} %get-tuple-element.91) | copy-start | bytes 9437188
  518.7 7.3 copy-start.11
  542.5 7.3 copy-start.25
  558.8 262.7 %reduce-scatter.5.cloned.1.call-start = ((), (), s32[]{:S(2)}) async-start(), calls=%async_computation.5 | async-start | bytes 7372800 | tf_op jit(solution)/shard_map/reduce_scatter | solution.py:239
  558.8 8.3 slice-start.4
  583.3 11.1 %copy-start.59 = (bf16[4,512,1024]{2,1,0:T(8,128)(2,1)S(1)}, bf16[4,512,1024]{2,1,0:T(8,128)(2,1)}, u32[]{:S(2)}) copy-start(bf16[4,512,1024]{2,1,0:T(8,128)(2,1)} %param.27) | copy-start | bytes 12582916
  583.3 19.3 %slice-start.6 = ((s8[6291456]{0:T(1024)(128)(4,1)}), s8[4194304]{0:T(1024)(128)(4,1)S(1)}, s32[]{:S(2)}) async-start(s8[6291456]{0:T(1024)(128)(4,1)} %bitcast.331), calls=%async_computation.13 | async-start | bytes 8388608
  594.4 8.2 slice-start.7
  608.2 12.0 %copy-start.51 = (f32[4,768]{1,0:T(4,128)S(1)}, f32[4,768]{1,0:T(4,128)}, u32[]{:S(2)}) copy-start(f32[4,768]{1,0:T(4,128)} %mul.775) | copy-start | bytes 36868
  647.8 14.7 %copy-start.49 = (f32[4,768]{1,0:T(4,128)S(1)}, f32[4,768]{1,0:T(4,128)}, u32[]{:S(2)}) copy-start(f32[4,768]{1,0:T(4,128)} %mul.766) | copy-start | bytes 36868
  662.5 15.8 %copy-start.28 = (f32[256,32]{1,0:T(8,128)S(1)}, f32[256,32]{1,0:T(8,128)}, u32[]{:S(2)}) copy-start(f32[256,32]{1,0:T(8,128)} %get-tuple-element.84) | copy-start | bytes 98308
  662.5 16.0 %copy-start.16 = (bf16[256,1024]{1,0:T(8,128)(2,1)S(1)}, bf16[256,1024]{1,0:T(8,128)(2,1)}, u32[]{:S(2)}) copy-start(bf16[256,1024]{1,0:T(8,128)(2,1)} %copy-done.15) | copy-start | bytes 1572868
  662.5 16.3 %copy-start.14 = (f32[256,1024]{1,0:T(8,128)S(1)}, f32[256,1024]{1,0:T(8,128)}, u32[]{:S(2)}) copy-start(f32[256,1024]{1,0:T(8,128)} %copy-done.13) | copy-start | bytes 3145732
  662.5 16.3 %copy-start.44 = (f32[1024]{0:T(1024)S(1)}, f32[1024]{0:T(1024)}, u32[]{:S(2)}) copy-start(f32[1024]{0:T(1024)} %copy-done.43) | copy-start | bytes 12292
  662.5 16.3 %copy-start.48 = (f32[256]{0:T(256)S(1)}, f32[256]{0:T(256)}, u32[]{:S(2)}) copy-start(f32[256]{0:T(256)} %copy-done.47) | copy-start | bytes 3076
  678.8 6.1 copy-start.34
  685.9 6.7 copy-start.36
  692.6 8.1 copy-start.40
  692.6 8.1 copy-start.42
  700.7 8.4 copy-start.32
  700.7 8.4 copy-start.37
  700.7 8.4 copy-start.38
  700.7 9.9 %copy-start.18 = (bf16[256,1024]{1,0:T(8,128)(2,1)S(1)}, bf16[256,1024]{1,0:T(8,128)(2,1)}, u32[]{:S(2)}) copy-start(bf16[256,1024]{1,0:T(8,128)(2,1)} %param.14) | copy-start | bytes 1572868
  700.7 9.9 %copy-start.46 = (f32[1024]{0:T(1024)S(1)}, f32[1024]{0:T(1024)}, u32[]{:S(2)}) copy-start(f32[1024]{0:T(1024)} %copy-done.45) | copy-start | bytes 12292
  710.6 8.1 copy-start.55
  724.4 15.3 %copy-start.6 = (bf16[4,768,512]{1,2,0:T(8,128)(2,1)S(1)}, bf16[4,768,512]{1,2,0:T(8,128)(2,1)}, u32[]{:S(2)}) copy-start(bf16[4,768,512]{1,2,0:T(8,128)(2,1)} %copy-done.5) | copy-start | bytes 9437188
  724.4 142.8 %all-reduce.4.cloned.1.call-start = ((), (), s32[]{:S(2)}) async-start(), calls=%async_computation.6 | async-start | bytes 1638400 | tf_op jit(solution)/shard_map/psum | solution.py:240
  739.7 9.8 %copy-start.52 = (f32[4,768]{1,0:T(4,128)S(1)}, f32[4,768]{1,0:T(4,128)}, u32[]{:S(2)}) copy-start(f32[4,768]{1,0:T(4,128)} %mul.775) | copy-start | bytes 36868
  766.8 17.1 %copy-start.8 = (bf16[4,768,512]{1,2,0:T(8,128)(2,1)S(1)}, bf16[4,768,512]{1,2,0:T(8,128)(2,1)}, u32[]{:S(2)}) copy-start(bf16[4,768,512]{1,2,0:T(8,128)(2,1)} %copy-done.7) | copy-start | bytes 9437188
  799.7 21.8 %copy-start.3 = (bf16[4,768,512]{1,2,0:T(8,128)(2,1)S(1)}, bf16[4,768,512]{1,2,0:T(8,128)(2,1)}, u32[]{:S(2)}) copy-start(bf16[4,768,512]{1,2,0:T(8,128)(2,1)} %copy-done.2) | copy-start | bytes 9437188
  821.5 15.4 %copy-start.56 = (f32[256]{0:T(256)S(1)}, f32[256]{0:T(256)}, u32[]{:S(2)}) copy-start(f32[256]{0:T(256)} %get-tuple-element.110) | copy-start | bytes 3076
  (23 other events, 88.6 us)
Sparse Core Ops, SparseCore 0:
  131.8 125.7 all-gather.2
  260.5 113.0 all-gather.4
  558.9 74.1 reduce-scatter.2
  724.5 63.5 reduce-scatter.4
  821.6 45.5 all-reduce.3
